TPU v7x, 32 devices: a whole 2x2x4 slice. The times are simulated.
32 devices in a mesh: row: 8 (over z, y), col: 4 (over x, core).
Axes of the slice: x: 2, y: 2, z: 4, core: 2. Of those that a mesh axis runs over, the one named last changes fastest.
Arguments:
- jacobian: float32 [16384, 16384], P('row', 'col'), may hold values from -6 to 6
- diff_inputs: float32 [32768, 128], P('row'), may hold values from -0.00390625 to 0.00390625
- diff_outputs: float32 [32768, 128], P('row'), may hold values from -6 to 6
- face_dof: int32 [32768], P('row'), may hold values from 0 to 16383, as said below
- counts: int32 [8], P('row'), may hold values from 128 to 4096, as said below
- residual: float32 [16384], P('col'), may hold values from -0.046875 to 0.046875
- trial: float32 [16384], P('row'), may hold values from -6 to 6
Outputs:
- updated: float32 [16384, 16384], P('row', 'col')
- corrected: float32 [16384], P('row')
Inputs may be any that keep to these rules, and one draw needn't show every extreme that they name: Each owner's count is a multiple of 128; the counts sum to 16384; some owner holds exactly 4096. `face_dof`: live slots name every degree of freedom exactly once over all owners, in runs of 128 consecutive degrees of freedom starting at multiples of 128; slots at or past an owner's count hold arbitrary values that belong to no column.
All inputs are finite; a program needn't handle non-finite values. Where the computation divides by a largest or mean magnitude, that divisor is 1e-20 or more.
Results may differ from a plain program's by a relative error of at most 0.0001.
Values sent between devices are 32-bit elements; how exact they have to be, the bound alone decides.
A program may use at most 192 MiB of HBM per device.

v0:
```python
import jax
import jax.numpy as jnp
from jax import lax
from jax.sharding import PartitionSpec as P

K = 128
NS = 4


HIGH = lax.Precision.HIGHEST
REG = 0.1


def ns_inverse(gram):
    eye = jnp.eye(K, dtype=jnp.float32)
    regular = gram + REG * (jnp.trace(gram) / K) * eye
    norm_one = jnp.max(jnp.sum(jnp.abs(regular), axis=0))
    iterate = regular / (norm_one * norm_one)
    for sweep in range(NS):
        iterate = jnp.dot(
            iterate, 2.0 * eye - jnp.dot(regular, iterate, precision=HIGH), precision=HIGH
        )
    return iterate


def per_device(jacobian, diff_inputs, diff_outputs, face_dof, counts, residual, trial):
    row_block, col_block = jacobian.shape
    row_count = lax.axis_size("row")
    total = row_block * row_count
    capacity = diff_inputs.shape[0]
    width = diff_inputs.shape[1]
    col_at = lax.axis_index("col")
    slots = jnp.arange(capacity, dtype=jnp.int32)
    live = slots < counts[0]
    masked = jnp.where(live[:, None], diff_inputs, 0.0)
    gram = lax.psum(jnp.dot(masked.T, masked, precision=HIGH), "row")
    target = jnp.where(live, face_dof, total)
    local = target - col_at * col_block
    inside = live & (local >= 0) & (local < col_block)
    place = jnp.where(inside, local, col_block)
    v_piece = jnp.zeros((col_block + 1, width), jnp.float32).at[place].set(diff_inputs)[:col_block]
    v_cols = lax.psum(v_piece, "row")
    w_piece = jnp.zeros((total + 1, width), jnp.float32).at[target].set(diff_outputs)[:total]
    w_rows = lax.psum_scatter(w_piece, "row", scatter_dimension=0, tiled=True)
    jv_part = jnp.dot(jacobian, v_cols, precision=HIGH)
    beta_part = jnp.dot(residual, v_cols, precision=HIGH)
    zmat = ns_inverse(gram)
    j_times_v, beta = lax.psum((jv_part, beta_part), "col")
    diff = w_rows - j_times_v
    updated = jacobian + jnp.dot(jnp.dot(diff, zmat, precision=HIGH), v_cols.T, precision=HIGH)
    applied = lax.psum(jnp.dot(updated, residual, precision=HIGH), "col")
    corrected = trial - applied
    return (updated, corrected)


def solution(mesh):
    placed = (
        P("row", "col"),
        P("row", None),
        P("row", None),
        P("row"),
        P("row"),
        P("col"),
        P("row"),
    )
    return jax.shard_map(
        per_device,
        mesh=mesh,
        in_specs=placed,
        out_specs=(P("row", "col"), P("row")),
        check_vma=False,
    )
```

profile of v0, /device:TPU:0, one launch (start us, length us, event | category | flops | bytes accessed | tf_op | source)
XLA Modules:
  0.0 433.8 jit_solution(5324949229296067871)
XLA Ops:
  7.2 0.0 copy-start
  7.2 0.0 all-reduce.6.cloned.1.call-start
  7.9 7.5 %fusion.2 = f32[128,128]{1,0:T(8,128)} fusion(f32[4096,128]{1,0:T(8,128)} %param.8, pred[4096]{0:T(1024)(128)(4,1)S(1)} %iota_compare_fusion.1), kind=kOutput, calls=%fused_computation.6 | convolution fusion | flops 805830656 | bytes 2166784 | tf_op jit(solution)/shard_map/dot_general | solution.py:36
  15.4 11.4 %scatter_custom_fusion.1 = f32[4097,128]{1,0:T(8,128)S(1)} fusion(s32[4096]{0:T(1024)S(1)} %get-tuple-element.5, f32[4096,128]{1,0:T(8,128)} %param.8, f32[]{:T(128)} %constant.10.clone.1), kind=kCustom, calls=%fused_computation.12 | custom fusion | bytes 2098176 | tf_op jit(solution)/shard_map/scatter | solution.py:41
  26.8 1.5 slice.9
  28.3 0.0 all-reduce.6.cloned.1.call-update
  28.3 0.0 all-reduce.4.cloned.1.call-start
  28.3 106.4 %all-reduce.6.cloned.1.call-done = (f32[128,128]{1,0:T(8,128)}, f32[4096,128]{1,0:T(8,128)}) async-done(((f32[128,128]{1,0:T(8,128)}, f32[4096,128]{1,0:T(8,128)}), (f32[128,128]{1,0:T(8,128)}, f32[4096,128]{1,0:T(8,128)})) %all-reduce.6.cloned.1.call-update) | async-done | bytes 2162704 | tf_op jit(solution)/shard_map/psum | solution.py:36
  134.7 31.5 %convolution_bitcast_fusion = f32[2048,128]{1,0:T(8,128)} fusion(f32[4096,128]{1,0:T(8,128)} %get-tuple-element.3, f32[2048,4096]{1,0:T(8,128)} %param.7), kind=kOutput, calls=%fused_computation.5 | convolution fusion | flops 12884901888 | bytes 36700160 | tf_op jit(solution)/shard_map/dot_general | solution.py:45
  166.2 0.0 all-reduce.4.cloned.1.call-update
  166.2 0.2 reduce-scatter.2.cloned.1.call-start
  166.5 14.8 %scatter_custom_fusion = f32[16385,128]{1,0:T(8,128)} fusion(s32[4096]{0:T(1024)S(1)} %get-tuple-element.4, f32[4096,128]{1,0:T(8,128)} %param.9, f32[]{:T(128)} %constant.10.clone.1), kind=kCustom, calls=%fused_computation.3 | custom fusion | bytes 8389632 | tf_op jit(solution)/shard_map/scatter | solution.py:43
  181.3 5.9 %slice.8 = f32[16384,128]{1,0:T(8,128)} slice(f32[16385,128]{1,0:T(8,128)} %scatter_custom_fusion), slice={[0:16384], [0:128]} | slice | bytes 16777216 | tf_op jit(solution)/shard_map/slice | solution.py:43
  187.2 0.0 reduce-scatter.2.cloned.1.call-update
  187.2 0.8 copy-done.2
  188.0 0.6 select_reduce_fusion
  189.3 0.6 reduce_max.9
  191.2 0.2 convolution_subtract_fusion.3
  191.5 0.2 fusion.10
  191.7 0.2 convolution_subtract_fusion.2
  191.9 0.2 fusion.21
  192.1 0.2 convolution_subtract_fusion.1
  192.3 0.2 fusion.22
  192.5 0.2 convolution_subtract_fusion
  192.8 0.2 fusion.23
  193.0 9.0 %all-reduce.4.cloned.1.call-done = f32[2048,128]{1,0:T(8,128)} async-done(((f32[2048,128]{1,0:T(8,128)}), f32[2048,128]{1,0:T(8,128)}) %all-reduce.4.cloned.1.call-update) | async-done | bytes 1048592 | tf_op jit(solution)/shard_map/psum | solution.py:48
  202.0 151.6 %reduce-scatter.2.cloned.1.call-done = f32[2048,128]{1,0:T(8,128)} async-done(((f32[16384,128]{1,0:T(8,128)}), f32[2048,128]{1,0:T(8,128)}) %reduce-scatter.2.cloned.1.call-update) | async-done | bytes 1048592 | tf_op jit(solution)/shard_map/reduce_scatter | solution.py:44
  353.6 2.5 fusion.7
  356.1 32.5 %convolution_add_fusion = f32[2048,4096]{1,0:T(8,128)} fusion(f32[2048,4096]{1,0:T(8,128)} %param.7, f32[2048,128]{1,0:T(8,128)S(1)} %fusion.7, f32[4096,128]{1,0:T(8,128)S(1)} %copy-done.1), kind=kOutput, calls=%fused_computation.2 | convolution fusion | flops 12893290496 | bytes 70254592 | tf_op jit(solution)/shard_map/dot_general | solution.py:50
  388.6 31.7 %fusion.24 = f32[1,2048]{1,0:T(1,128)S(1)} fusion(f32[2048,4096]{1,0:T(8,128)} %convolution_add_fusion, f32[4096,1]{0,1:T(1,128)S(1)} %bitcast.26), kind=kOutput, calls=%fused_computation.39 | convolution fusion | flops 100663296 | bytes 33579008 | tf_op jit(solution)/shard_map/dot_general | solution.py:51
  420.3 6.4 %psum.31 = f32[2048]{0:T(1024)S(1)} all-reduce(f32[2048]{0:T(1024)S(1)} %bitcast.27), channel_id=1, replica_groups=mesh['row'=8,'col'=4] {'col'}, use_global_device_ids=true, to_apply=%region_9.10 | all-reduce | flops 2048 | bytes 16384 | tf_op jit(solution)/shard_map/psum | solution.py:51
  426.7 0.6 sub.31
  (11 shorter events, 0.1 us)
Async XLA Ops:
  7.2 381.5 %copy-start = (f32[4096]{0:T(1024)S(1)}, f32[4096]{0:T(1024)}, u32[]{:S(2)}) copy-start(f32[4096]{0:T(1024)} %param.12) | copy-start | bytes 49156
  7.2 8.2 %copy-start.3 = (s32[4096]{0:T(1024)S(1)}, s32[4096]{0:T(1024)}, u32[]{:S(2)}) copy-start(s32[4096]{0:T(1024)} %param.10) | copy-start | bytes 49156
  7.2 127.5 %all-reduce.6.cloned.1.call-start = ((), (), s32[]{:S(2)}) async-start(), calls=%async_computation.3 | async-start | bytes 4325376 | tf_op jit(solution)/shard_map/psum | solution.py:36
  28.3 173.7 %all-reduce.4.cloned.1.call-start = ((), (), s32[]{:S(2)}) async-start(), calls=%async_computation.2 | async-start | bytes 2097152 | tf_op jit(solution)/shard_map/psum | solution.py:48
  166.2 187.3 %reduce-scatter.2.cloned.1.call-start = ((), (), s32[]{:S(2)}) async-start(), calls=%async_computation.1 | async-start | bytes 9437184 | tf_op jit(solution)/shard_map/reduce_scatter | solution.py:44
  187.2 0.8 copy-start.2
  191.9 164.2 %copy-start.1 = (f32[4096,128]{1,0:T(8,128)S(1)}, f32[4096,128]{1,0:T(8,128)}, u32[]{:S(2)}) copy-start(f32[4096,128]{1,0:T(8,128)} %get-tuple-element.3) | copy-start | bytes 6291460
  388.6 38.1 %copy-start.4 = (f32[2048]{0:T(1024)S(1)}, f32[2048]{0:T(1024)}, u32[]{:S(2)}) copy-start(f32[2048]{0:T(1024)} %param.13) | copy-start | bytes 24580
Sparse Core Ops, SparseCore 0:
  28.4 106.2 all-reduce.5
  166.4 35.5 all-reduce.3
  205.6 147.8 reduce-scatter.1
where the time goes:
time: 434 us
  waiting for transfers between devices  267 us (62%)
  matrix products  107 us (25%)
  local copies, waits for them, and re-layouts  34.4 us (8%)
  between operations  16.5 us (4%)
  blocking collectives  6.38 us (1%)
    reduce_scatter x1, waiting for transfers between devices, per_device(): w_rows = lax.psum_scatter(w_piece, 'row', scatter_dimension=0, tiled=True)  152 us
    psum x1, waiting for transfers between devices, per_device(): gram = lax.psum(jnp.dot(masked.T, masked, precision=HIGH), 'row')  106 us
    dot_general x1, matrix products, per_device(): jnp.dot(jnp.dot(diff, zmat, precision=HIGH), v_cols.T, precision=HIGH)  32.5 us
    dot_general x1, matrix products, per_device(): applied = lax.psum(jnp.dot(updated, residual, precision=HIGH), 'col')  31.7 us
    dot_general x1, matrix products, per_device(): jv_part = jnp.dot(jacobian, v_cols, precision=HIGH)  31.5 us
    scatter x1, local copies, waits for them, and re-layouts, per_device(): jnp.zeros((total + 1, width), jnp.float32).at[target].set(diff_outputs)  14.8 us
    scatter x1, local copies, waits for them, and re-layouts, per_device(): jnp.zeros((col_block + 1, width), jnp.float32).at[place].set(diff_inputs)  11.4 us
    psum x1, waiting for transfers between devices, per_device(): j_times_v, beta = lax.psum((jv_part, beta_part), 'col')  9.04 us
  transfers between devices with their start and end apart: 3, of which 3 were waited for; matrix products, arithmetic and copies ran while one was open for 5% of the time, Pallas kernels for 0%

commit v1 on v0

v1 whole, which is shorter than its diff:
```python
import functools

import jax
import jax.numpy as jnp
from jax import lax
from jax.experimental import pallas as pl
from jax.experimental.pallas import tpu as pltpu
from jax.sharding import PartitionSpec as P

K = 128
NS = 4
UNIT = 128
TILE = 256

HIGH = lax.Precision.HIGHEST
REG = 0.1
F32 = jnp.float32
BF16 = jnp.bfloat16
MESH = pl.DeviceIdType.MESH
VMEM_SPEC = pl.BlockSpec(memory_space=pltpu.VMEM)
SMEM_SPEC = pl.BlockSpec(memory_space=pltpu.SMEM)


def ns_inverse(gram):
    eye = jnp.eye(K, dtype=F32)
    regular = gram + REG * (jnp.trace(gram) / K) * eye
    norm_one = jnp.max(jnp.sum(jnp.abs(regular), axis=0))
    iterate = regular / (norm_one * norm_one)
    for sweep in range(NS):
        iterate = jnp.dot(
            iterate, 2.0 * eye - jnp.dot(regular, iterate, precision=HIGH), precision=HIGH
        )
    return iterate


def split(x):
    hi = x.astype(BF16)
    return hi, (x - hi.astype(F32)).astype(BF16)


def ring_place(index, n):
    return index // 2 + (index % 2) * (n - 1 - 2 * (index // 2))


def ring_index(place, n):
    side = place // (n // 2)
    level = place + side * (n - 1 - 2 * place)
    return 2 * level + side


def ring_kernel(n, parts, src_ref, mask_ref, x_ref, out_ref, landed, sent, send_sem, recv_sem):
    place = ring_place(lax.axis_index("row"), n)
    right = ring_index((place + 1) % n, n)
    left = ring_index((place + n - 1) % n, n)
    barrier = pltpu.get_barrier_semaphore()
    for peer in (left, right):
        pl.semaphore_signal(barrier, inc=1, device_id={"row": peer}, device_id_type=MESH)
    pl.semaphore_wait(barrier, 2)

    def granule(way, back, part):
        sign = 1 if way == 0 else -1
        chunk = (place + 2 * n - sign * back) % n
        return (way * n + chunk) * parts + part

    def own(at):
        return x_ref[src_ref[at]] * mask_ref[at]

    def copy(step, way, part, source, target):
        return pltpu.make_async_remote_copy(
            src_ref=source,
            dst_ref=target,
            send_sem=send_sem.at[way, step, part],
            recv_sem=recv_sem.at[way, step, part],
            device_id={"row": right if way == 0 else left},
            device_id_type=MESH,
        )

    copies = {}
    last = 2 * (n - 1)
    for step in range(last + 1):
        for part in range(parts):
            for way in range(2):
                if step > 0:
                    copies[step - 1, way, part].wait_recv()
                if step < n - 1:
                    at = granule(way, step, part)
                    value = own(at)
                    if step > 0:
                        value = value + landed[way, step - 1, part]
                    sent[way, step, part] = value
                    source, target = sent.at[way, step, part], landed.at[way, step, part]
                elif step < last:
                    at = granule(way, step, part)
                    if step == n - 1:
                        out_ref[at] = own(at) + landed[way, step - 1, part]
                    source, target = out_ref.at[at], out_ref.at[at]
                else:
                    continue
                copies[step, way, part] = copy(step, way, part, source, target)
                copies[step, way, part].start()
    for key in copies:
        copies[key].wait_send()


def ring_sum(src, mask, x, rows, n):
    chunk = rows // (2 * n)
    part = min(UNIT, chunk)
    parts = chunk // part
    granules = rows // part
    return pl.pallas_call(
        functools.partial(ring_kernel, n, parts),
        out_shape=jax.ShapeDtypeStruct((granules, part, K), F32),
        in_specs=[SMEM_SPEC, SMEM_SPEC, VMEM_SPEC],
        out_specs=VMEM_SPEC,
        scratch_shapes=[
            pltpu.VMEM((2, n - 1, parts, part, K), F32),
            pltpu.VMEM((2, n - 1, parts, part, K), F32),
            pltpu.SemaphoreType.DMA((2, 2 * (n - 1), parts)),
            pltpu.SemaphoreType.DMA((2, 2 * (n - 1), parts)),
        ],
        compiler_params=pltpu.CompilerParams(collective_id=0, has_side_effects=True),
    )(src, mask, x.reshape(-1, part, K)).reshape(rows, K)


def lookup(run_unit, wanted):
    hit = run_unit[None, :] == wanted[:, None]
    src = jnp.sum(jnp.where(hit, jnp.arange(run_unit.shape[0], dtype=jnp.int32)[None, :], 0), axis=1)
    return src.astype(jnp.int32), jnp.any(hit, axis=1).astype(F32)


def place_kernel(src_ref, mask_ref, x_ref, out_ref):
    for unit in range(out_ref.shape[0]):
        out_ref[unit] = x_ref[src_ref[unit]] * mask_ref[unit]


def place_units(src, mask, x):
    return pl.pallas_call(
        place_kernel,
        out_shape=jax.ShapeDtypeStruct((src.shape[0], UNIT, K), F32),
        in_specs=[SMEM_SPEC, SMEM_SPEC, VMEM_SPEC],
        out_specs=VMEM_SPEC,
    )(src, mask, x.reshape(-1, UNIT, K)).reshape(-1, K)


def product_kernel(j_ref, v_ref, r_ref, jv_ref, jr_ref, gram_ref, beta_ref, vb):
    @pl.when(pl.program_id(0) == 0)
    def _():
        hi, lo = split(v_ref[...])
        vb[:, :K] = hi
        vb[:, K:] = lo
        both = vb[...]
        full = lax.dot_general(both, both, (((0,), (0,)), ((), ())), preferred_element_type=F32)
        gram_ref[...] = full[:K, :K] + (full[:K, K:] + full[K:, :K]) + full[K:, K:]
        rows = jnp.broadcast_to(r_ref[...], (8, r_ref.shape[1]))
        r_hi, r_lo = split(rows)
        b_hi = jnp.dot(r_hi, both, preferred_element_type=F32)
        b_lo = jnp.dot(r_lo, both, preferred_element_type=F32)
        beta_ref[...] = b_hi[:, :K] + (b_hi[:, K:] + b_lo[:, :K])

    tile = j_ref[...]
    hi, lo = split(tile)
    main = jnp.dot(hi, vb[...], preferred_element_type=F32)
    rest = jnp.dot(lo, vb[:, :K], preferred_element_type=F32)
    jv_ref[...] = main[:, :K] + (main[:, K:] + rest)
    total = jnp.zeros((tile.shape[0], K), F32)
    for at in range(0, tile.shape[1], K):
        total = total + j_ref[:, at : at + K] * r_ref[:, at : at + K]
    jr_ref[...] = jnp.sum(jnp.transpose(total), axis=0, keepdims=True)


def products(jacobian, v_cols, residual):
    rows, cols = jacobian.shape
    return pl.pallas_call(
        product_kernel,
        grid=(rows // TILE,),
        out_shape=(
            jax.ShapeDtypeStruct((rows, K), F32),
            jax.ShapeDtypeStruct((1, rows), F32),
            jax.ShapeDtypeStruct((K, K), F32),
            jax.ShapeDtypeStruct((8, K), F32),
        ),
        in_specs=[
            pl.BlockSpec((TILE, cols), lambda i: (i, 0)),
            pl.BlockSpec((cols, K), lambda i: (0, 0)),
            pl.BlockSpec((1, cols), lambda i: (0, 0)),
        ],
        out_specs=(
            pl.BlockSpec((TILE, K), lambda i: (i, 0)),
            pl.BlockSpec((1, TILE), lambda i: (0, i)),
            pl.BlockSpec((K, K), lambda i: (0, 0)),
            pl.BlockSpec((8, K), lambda i: (0, 0)),
        ),
        scratch_shapes=[pltpu.VMEM((cols, 2 * K), BF16)],
    )(jacobian, v_cols, residual.reshape(1, cols))


def update_kernel(j_ref, u_ref, vt_ref, out_ref):
    hi, lo = split(u_ref[...])
    twice = jnp.concatenate([hi, hi], axis=1)
    main = jnp.dot(twice, vt_ref[...], preferred_element_type=F32)
    rest = jnp.dot(lo, vt_ref[:K, :], preferred_element_type=F32)
    out_ref[...] = j_ref[...] + (main + rest)


def update(jacobian, u_rows, vt):
    rows, cols = jacobian.shape
    return pl.pallas_call(
        update_kernel,
        grid=(rows // TILE,),
        out_shape=jax.ShapeDtypeStruct((rows, cols), F32),
        in_specs=[
            pl.BlockSpec((TILE, cols), lambda i: (i, 0)),
            pl.BlockSpec((TILE, K), lambda i: (i, 0)),
            pl.BlockSpec((2 * K, cols), lambda i: (0, 0)),
        ],
        out_specs=pl.BlockSpec((TILE, cols), lambda i: (i, 0)),
    )(jacobian, u_rows, vt)


def per_device(jacobian, diff_inputs, diff_outputs, face_dof, counts, residual, trial):
    row_block, col_block = jacobian.shape
    n_row, n_col = lax.axis_size("row"), lax.axis_size("col")
    col_at = lax.axis_index("col")
    runs = face_dof.shape[0] // UNIT
    first = jnp.arange(runs, dtype=jnp.int32) * UNIT
    run_unit = jnp.where(first < counts[0], face_dof.reshape(runs, UNIT)[:, 0] // UNIT, -1)

    part = min(UNIT, col_block // (2 * n_row))
    per_unit = UNIT // part
    granule = jnp.arange(col_block // part, dtype=jnp.int32)
    v_src, v_mask = lookup(run_unit, col_at * (col_block // UNIT) + granule // per_unit)
    v_src = v_src * per_unit + granule % per_unit
    v_cols = ring_sum(v_src, v_mask, diff_inputs, col_block, n_row)

    share = row_block // n_col // UNIT
    unit = jnp.arange(n_row * share, dtype=jnp.int32)
    w_unit = (unit // share) * (row_block // UNIT) + col_at * share + unit % share
    w_src, w_mask = lookup(run_unit, w_unit)
    w_piece = place_units(w_src, w_mask, diff_outputs)
    w_rows = lax.psum_scatter(w_piece, "row", scatter_dimension=0, tiled=True)

    jv_part, jr_part, gram_part, beta_part = products(jacobian, v_cols, residual)
    jv_rows = lax.psum_scatter(jv_part, "col", scatter_dimension=0, tiled=True)
    gram, beta, j_r = lax.psum((gram_part, beta_part, jr_part), "col")
    zmat = ns_inverse(gram)
    u_share = jnp.dot(w_rows - jv_rows, zmat, precision=HIGH)
    u_rows = lax.all_gather(u_share, "col", axis=0, tiled=True)
    v_t = v_cols.T
    vt_hi = lax.reduce_precision(v_t, 8, 7)
    vt = jnp.concatenate([vt_hi.astype(BF16), (v_t - vt_hi).astype(BF16)], axis=0)
    updated = update(jacobian, u_rows, vt)
    corrected = trial - (j_r[0] + jnp.dot(u_rows, beta[0], precision=HIGH))
    return (updated, corrected)


def solution(mesh):
    placed = (
        P("row", "col"),
        P("row", None),
        P("row", None),
        P("row"),
        P("row"),
        P("col"),
        P("row"),
    )
    return jax.shard_map(
        per_device,
        mesh=mesh,
        in_specs=placed,
        out_specs=(P("row", "col"), P("row")),
        check_vma=False,
    )
```

time: 434 us -> 276 us (0.64)
  waiting for transfers between devices: 267 us -> 116 us
  Pallas kernels: 0 us -> 110 us
  matrix products: 107 us -> 10.3 us
  local copies, waits for them, and re-layouts: 34.4 us -> 2.66 us
  other arithmetic: 1.88 us -> 9.29 us
  blocking collectives: 6.38 us -> 10.9 us
    pallas_call x0 -> x4, Pallas kernels: none -> 110 us  [the longest x1 61 us: ring_sum(): pl.pallas_call(functools.partial(ring_kernel, n, parts), out_shape=jax.Sh...]
    dot_general x5 -> x2, matrix products: 106 us -> 4.34 us  [the longest x1 2.2 us: per_device(): corrected = trial - (j_r[0] + jnp.dot(u_rows, beta[0], precision=HIGH))]
    psum x2 -> x1, waiting for transfers between devices: 115 us -> 26.2 us  [per_device(): gram, beta, j_r = lax.psum((gram_part, beta_part, jr_part), 'col')]
    reduce_scatter x1, waiting for transfers between devices: 152 us -> 72.5 us  [per_device(): w_rows = lax.psum_scatter(w_piece, 'row', scatter_dimension=0, tiled=True)]
    scatter x2 -> x0, local copies, waits for them, and re-layouts: 26.2 us -> none  [the longest x1 14.8 us: per_device(): jnp.zeros((total + 1, width), jnp.float32).at[target].set(diff_outputs)]
    reduce_scatter x0 -> x1, waiting for transfers between devices: none -> 16.2 us  [per_device(): jv_rows = lax.psum_scatter(jv_part, 'col', scatter_dimension=0, tiled=True)]
    slice x2 -> x1, local copies, waits for them, and re-layouts: 7.35 us -> 0.83 us  [per_device(): face_dof.reshape(runs, UNIT)[:, 0] // UNIT]
    psum x1, blocking collectives: 6.38 us -> 10.9 us  [per_device(): gram, beta, j_r = lax.psum((gram_part, beta_part, jr_part), 'col')]
  transfers between devices with their start and end apart: 3 -> 4, of which waited for: 3 -> 3; matrix products, arithmetic and copies ran while one was open for 5% -> 5% of each run, Pallas kernels for 0% -> 1%
where the time goes in v1:
time: 276 us
  waiting for transfers between devices  116 us (42%)
  Pallas kernels  110 us (40%)
  between operations  16.6 us (6%)
  blocking collectives  10.9 us (4%)
  matrix products  10.3 us (4%)
  other arithmetic  9.29 us (3%)
    reduce_scatter x1, waiting for transfers between devices, per_device(): w_rows = lax.psum_scatter(w_piece, 'row', scatter_dimension=0, tiled=True)  72.5 us
    pallas_call x1, Pallas kernels, ring_sum(): pl.pallas_call(functools.partial(ring_kernel, n, parts), out_shape=jax.Sh...  61 us
    pallas_call x1, Pallas kernels, update(): pl.pallas_call(update_kernel, grid=(rows // TILE,), out_shape=jax.ShapeDt...  26.6 us
    psum x1, waiting for transfers between devices, per_device(): gram, beta, j_r = lax.psum((gram_part, beta_part, jr_part), 'col')  26.2 us
    pallas_call x1, Pallas kernels, products(): pl.pallas_call(product_kernel, grid=(rows // TILE,), out_shape=(jax.Shape...  19.3 us
    reduce_scatter x1, waiting for transfers between devices, per_device(): jv_rows = lax.psum_scatter(jv_part, 'col', scatter_dimension=0, tiled=True)  16.2 us
    psum x1, blocking collectives, per_device(): gram, beta, j_r = lax.psum((gram_part, beta_part, jr_part), 'col')  10.9 us
  transfers between devices with their start and end apart: 4, of which 3 were waited for; matrix products, arithmetic and copies ran while one was open for 5% of the time, Pallas kernels for 1%

profile of v1, /device:TPU:0, one launch (start us, length us, event | category | flops | bytes accessed | tf_op | source)
XLA Modules:
  0.0 275.6 jit_solution(3723636031850268505)
XLA Ops:
  7.9 0.8 slice_reduce_fusion
  8.7 0.2 compare_reduce_fusion.1
  8.9 0.8 fusion.8
  9.7 0.5 convert_element_type.14.mask_ref
  10.2 61.0 %shard_map.87 = f32[32,128,128]{2,1,0:T(8,128)} custom-call(s32[32]{0:T(128)} %get-tuple-element.13.src_ref, f32[32]{0:T(128)} %convert_element_type.14.mask_ref, f32[32,128,128]{2,1,0:T(8,128)} %bitcast.32), custom_call_target="tpu_custom_call" | custom-call | tf_op jit(solution)/shard_map/pallas_call | solution.py:110
  71.2 19.3 %shard_map.88 = (f32[2048,128]{1,0:T(8,128)}, f32[1,2048]{1,0:T(1,128)}, f32[128,128]{1,0:T(8,128)}, f32[8,128]{1,0:T(8,128)}) custom-call(f32[2048,4096]{1,0:T(8,128)} %j_ref.3, f32[4096,128]{1,0:T(8,128)} %bitcast.29, f32[1,4096]{1,0:T(1,128)} %bitcast.35), custom_call_target="tpu_custom_call" | custom-call | tf_op jit(solution)/shard_map/pallas_call | solution.py:173
  90.6 0.7 reduce-scatter.5.cloned.1.call-update
  91.3 0.6 convert_element_type.13.mask_ref
  91.9 3.1 %shard_map.86 = f32[32,128,128]{2,1,0:T(8,128)} custom-call(s32[32]{0:T(128)} %get-tuple-element.12.src_ref, f32[32]{0:T(128)} %convert_element_type.13.mask_ref, f32[32,128,128]{2,1,0:T(8,128)} %bitcast.33), custom_call_target="tpu_custom_call" | custom-call | tf_op jit(solution)/shard_map/pallas_call | solution.py:137
  95.0 0.0 all-gather.2.cloned.1.call-start
  95.1 26.2 %all-reduce.3.cloned.1.call-done = f32[128,128]{1,0:T(8,128)} async-done(((f32[128,128]{1,0:T(8,128)}), f32[128,128]{1,0:T(8,128)}) %all-reduce.3.cloned.1.call-update) | async-done | bytes 65552 | tf_op jit(solution)/shard_map/psum | solution.py:244
  121.3 1.5 select_reduce_fusion
  123.5 0.9 abs_reduce_fusion
  124.4 0.7 reduce_max.9
  126.5 1.1 convolution_subtract_fusion.3
  127.6 1.1 fusion.3
  128.6 1.1 convolution_subtract_fusion.2
  129.7 0.2 fusion.21
  129.9 1.1 convolution_subtract_fusion.1
  131.0 0.2 fusion.22
  131.2 1.1 convolution_subtract_fusion
  132.3 0.2 fusion.23
  132.5 16.2 %reduce-scatter.5.cloned.1.call-done = f32[512,128]{1,0:T(8,128)} async-done(((f32[2048,128]{1,0:T(8,128)}), f32[512,128]{1,0:T(8,128)}) %reduce-scatter.5.cloned.1.call-update) | async-done | bytes 262160 | tf_op jit(solution)/shard_map/reduce_scatter | solution.py:243
  148.6 72.5 %reduce-scatter.3.cloned.1.call-done = f32[512,128]{1,0:T(8,128)} async-done(((f32[4096,128]{1,0:T(8,128)}), f32[512,128]{1,0:T(8,128)}) %reduce-scatter.3.cloned.1.call-update) | async-done | bytes 262160 | tf_op jit(solution)/shard_map/reduce_scatter | solution.py:240
  221.1 2.1 fusion.1
  223.3 1.8 copy.17
  225.1 10.9 %all-reduce = (f32[2048]{0:T(1024)S(1)}, f32[8,128]{1,0:T(8,128)S(1)}) all-reduce(f32[2048]{0:T(1024)S(1)} %bitcast.37, f32[8,128]{1,0:T(8,128)S(1)} %copy-done.3), channel_id=1, replica_groups=mesh['row'=8,'col'=4] {'col'}, use_global_device_ids=true, to_apply=%region_10.11 | all-reduce | flops 3072 | bytes 24576 | tf_op jit(solution)/shard_map/psum | solution.py:244
  236.1 1.9 reduce-precision_convert_fusion
  238.0 1.6 pad_maximum_fusion.vt_ref
  239.6 2.2 fusion.13
  241.8 0.6 add_subtract_fusion
  242.4 26.6 %shard_map.89 = f32[2048,4096]{1,0:T(8,128)} custom-call(f32[2048,4096]{1,0:T(8,128)} %j_ref.3, f32[2048,128]{1,0:T(8,128)} %all-gather.2.cloned.1.call-done.u_ref, bf16[256,4096]{1,0:T(8,128)(2,1)} %pad_maximum_fusion.vt_ref), custom_call_target="tpu_custom_call" | custom-call | tf_op jit(solution)/shard_map/pallas_call | solution.py:207
  (17 shorter events, 0.2 us)
Async XLA Ops:
  7.2 114.1 %all-reduce.3.cloned.1.call-start = ((), (), s32[]{:S(2)}) async-start(), calls=%async_computation.4 | async-start | bytes 131072 | tf_op jit(solution)/shard_map/psum | solution.py:244
  90.5 58.1 %reduce-scatter.5.cloned.1.call-start = ((), (), s32[]{:S(2)}) async-start(), calls=%async_computation.3 | async-start | bytes 1310720 | tf_op jit(solution)/shard_map/reduce_scatter | solution.py:243
  91.3 129.8 %reduce-scatter.3.cloned.1.call-start = ((), (), s32[]{:S(2)}) async-start(), calls=%async_computation.2 | async-start | bytes 2359296 | tf_op jit(solution)/shard_map/reduce_scatter | solution.py:240
  95.0 128.3 %copy-start = (f32[32,128,128]{2,1,0:T(8,128)S(1)}, f32[32,128,128]{2,1,0:T(8,128)}, u32[]{:S(2)}) copy-start(f32[32,128,128]{2,1,0:T(8,128)} %shard_map.87) | copy-start | bytes 6291460
  95.0 144.6 %all-gather.2.cloned.1.call-start = ((), (), s32[]{:S(2)}) async-start(), calls=%async_computation.5 | async-start | bytes 1310720 | tf_op jit(solution)/shard_map/all_gather | solution.py:247
  223.3 1.8 copy-start.1
  223.3 1.8 copy-start.3
  238.0 3.8 %copy-start.2 = (f32[2048]{0:T(1024)S(1)}, f32[2048]{0:T(1024)}, u32[]{:S(2)}) copy-start(f32[2048]{0:T(1024)} %param.13) | copy-start | bytes 24580
Sparse Core Ops, SparseCore 0:
  90.7 30.5 all-reduce.2
  123.8 24.7 reduce-scatter.4
  152.7 68.3 reduce-scatter.2
  223.4 15.8 all-gather.1

commit v2 on v1

v2 whole, which is shorter than its diff:
```python
import functools

import jax
import jax.numpy as jnp
from jax import lax
from jax.experimental import pallas as pl
from jax.experimental.pallas import tpu as pltpu
from jax.sharding import PartitionSpec as P

K = 128
NS = 4
UNIT = 128
TILE = 256

HIGH = lax.Precision.HIGHEST
REG = 0.1
F32 = jnp.float32
BF16 = jnp.bfloat16
MESH = pl.DeviceIdType.MESH
VMEM_SPEC = pl.BlockSpec(memory_space=pltpu.VMEM)
SMEM_SPEC = pl.BlockSpec(memory_space=pltpu.SMEM)


def split(x):
    hi = x.astype(BF16)
    return hi, (x - hi.astype(F32)).astype(BF16)


def ring_place(index, n):
    return index // 2 + (index % 2) * (n - 1 - 2 * (index // 2))


def ring_index(place, n):
    side = place // (n // 2)
    level = place + side * (n - 1 - 2 * place)
    return 2 * level + side


def ring_kernel(
    n, parts, src_ref, mask_ref, x_ref, r_ref, vb_ref, vt_ref, gb_ref,
    whole, landed, sent, gram, beta, send_sem, recv_sem,
):
    place = ring_place(lax.axis_index("row"), n)
    right = ring_index((place + 1) % n, n)
    left = ring_index((place + n - 1) % n, n)
    barrier = pltpu.get_barrier_semaphore()
    for peer in (left, right):
        pl.semaphore_signal(barrier, inc=1, device_id={"row": peer}, device_id_type=MESH)
    pl.semaphore_wait(barrier, 2)

    def granule(way, back, part):
        sign = 1 if way == 0 else -1
        chunk = (place + 2 * n - sign * back) % n
        return (way * n + chunk) * parts + part

    def own(at):
        return x_ref[src_ref[at]] * mask_ref[at]

    def copy(step, way, part, source, target):
        return pltpu.make_async_remote_copy(
            src_ref=source,
            dst_ref=target,
            send_sem=send_sem.at[way, step, part],
            recv_sem=recv_sem.at[way, step, part],
            device_id={"row": right if way == 0 else left},
            device_id_type=MESH,
        )

    per_unit = UNIT // whole.shape[1]

    def absorb(unit):
        rows = jnp.concatenate([whole[unit * per_unit + sub] for sub in range(per_unit)], axis=0)
        at = pl.ds(pl.multiple_of(unit * UNIT, UNIT), UNIT)
        hi, lo = split(rows)
        both = jnp.concatenate([hi, lo], axis=1)
        vb_ref[at, :] = both
        t_hi, t_lo = split(jnp.transpose(rows))
        vt_ref[:K, at] = t_hi
        vt_ref[K:, at] = t_lo
        gram[...] += lax.dot_general(
            both, both, (((0,), (0,)), ((), ())), preferred_element_type=F32
        )
        r_hi, r_lo = split(jnp.broadcast_to(r_ref[:, at], (8, UNIT)))
        beta[...] += jnp.dot(
            jnp.concatenate([r_hi, r_lo], axis=0), both, preferred_element_type=F32
        )

    gram[...] = jnp.zeros_like(gram)
    beta[...] = jnp.zeros_like(beta)
    copies = {}
    last = 2 * (n - 1)
    for step in range(last + 1):
        for part in range(parts):
            for way in range(2):
                if step > 0:
                    copies[step - 1, way, part].wait_recv()
                at = granule(way, step, part)
                if step < n - 1:
                    value = own(at)
                    if step > 0:
                        value = value + landed[way, step - 1, part]
                    sent[way, step, part] = value
                    source, target = sent.at[way, step, part], landed.at[way, step, part]
                else:
                    if step == n - 1:
                        whole[at] = own(at) + landed[way, step - 1, part]
                    source, target = whole.at[at], whole.at[at]
                if step < last:
                    copies[step, way, part] = copy(step, way, part, source, target)
                    copies[step, way, part].start()
                if step >= n - 1 and per_unit == 1:
                    absorb(at)
    if per_unit > 1:
        for unit in range(whole.shape[0] // per_unit):
            absorb(unit)
    gb_ref[:K, :] = gram[:K, :K] + (gram[:K, K:] + gram[K:, :K]) + gram[K:, K:]
    gb_ref[K:, :] = beta[:8, :K] + (beta[:8, K:] + beta[8:, :K])
    for key in copies:
        copies[key].wait_send()


def ring_sum(src, mask, x, residual, rows, n):
    chunk = rows // (2 * n)
    part = min(UNIT, chunk)
    parts = chunk // part
    return pl.pallas_call(
        functools.partial(ring_kernel, n, parts),
        out_shape=(
            jax.ShapeDtypeStruct((rows, 2 * K), BF16),
            jax.ShapeDtypeStruct((2 * K, rows), BF16),
            jax.ShapeDtypeStruct((K + 8, K), F32),
        ),
        in_specs=[SMEM_SPEC, SMEM_SPEC, VMEM_SPEC, VMEM_SPEC],
        out_specs=(VMEM_SPEC, VMEM_SPEC, VMEM_SPEC),
        scratch_shapes=[
            pltpu.VMEM((rows // part, part, K), F32),
            pltpu.VMEM((2, n - 1, parts, part, K), F32),
            pltpu.VMEM((2, n - 1, parts, part, K), F32),
            pltpu.VMEM((2 * K, 2 * K), F32),
            pltpu.VMEM((16, 2 * K), F32),
            pltpu.SemaphoreType.DMA((2, 2 * (n - 1), parts)),
            pltpu.SemaphoreType.DMA((2, 2 * (n - 1), parts)),
        ],
        compiler_params=pltpu.CompilerParams(collective_id=0, has_side_effects=True),
    )(src, mask, x.reshape(-1, part, K), residual)


def lookup(run_unit, wanted):
    hit = run_unit[None, :] == wanted[:, None]
    src = jnp.sum(jnp.where(hit, jnp.arange(run_unit.shape[0], dtype=jnp.int32)[None, :], 0), axis=1)
    return src.astype(jnp.int32), jnp.any(hit, axis=1).astype(F32)


def product_kernel(
    n, nc, parts, src_ref, mask_ref, x_ref, gb_ref, r_ref, vb_ref, j_ref,
    u_ref, beta_ref, jr_ref,
    w_land, w_sent, w_share, jv, jv_land, jr_all, gb_all, u_all,
    w_send, w_recv, jv_send, jv_recv, gb_send, gb_recv, jr_send, jr_recv, u_send, u_recv,
):
    tiles = jr_all.shape[1]
    tile = jr_all.shape[2]
    share = jv_land.shape[1]
    per_share = share // tile
    grain = w_share.shape[2]
    step_now = pl.program_id(0)
    me = lax.axis_index("col")
    place = ring_place(lax.axis_index("row"), n)
    right = ring_index((place + 1) % n, n)
    left = ring_index((place + n - 1) % n, n)
    peers = [(me + k) % nc for k in range(1, nc)]

    def to_col(source, target, send, recv, peer):
        return pltpu.make_async_remote_copy(
            src_ref=source, dst_ref=target, send_sem=send, recv_sem=recv,
            device_id={"col": peer}, device_id_type=MESH,
        )

    def gb_copy(k, slot):
        return to_col(gb_ref, gb_all.at[slot], gb_send.at[k], gb_recv.at[slot], peers[k])

    def jr_copy(k, slot):
        return to_col(jr_all.at[slot], jr_all.at[slot], jr_send.at[k], jr_recv.at[slot], peers[k])

    def jv_copy(at, sender, owner):
        rows = pl.ds(pl.multiple_of((at % per_share) * tile, tile), tile)
        return to_col(
            jv.at[at], jv_land.at[sender, rows], jv_send.at[at],
            jv_recv.at[sender, at % per_share], owner,
        )

    def w_copy(step, way, part):
        return pltpu.make_async_remote_copy(
            src_ref=w_sent.at[way, step, part], dst_ref=w_land.at[way, step, part],
            send_sem=w_send.at[way, step, part], recv_sem=w_recv.at[way, step, part],
            device_id={"row": right if way == 0 else left}, device_id_type=MESH,
        )

    def w_step(step):
        for part in range(parts):
            for way in range(2):
                sign = 1 if way == 0 else -1
                block = ring_index((place + 2 * n - sign * (step + 1)) % n, n)
                at = (block * 2 + way) * parts + part
                value = x_ref[src_ref[at]] * mask_ref[at]
                if step > 0:
                    w_copy(step - 1, way, part).wait_recv()
                    value = value + w_land[way, step - 1, part]
                if step < n - 1:
                    w_sent[way, step, part] = value
                    w_copy(step, way, part).start()
                else:
                    w_share[way, part] = value

    @pl.when(step_now == 0)
    def _():
        barrier = pltpu.get_barrier_semaphore()
        for peer in (left, right):
            pl.semaphore_signal(barrier, inc=1, device_id={"row": peer}, device_id_type=MESH)
        for peer in peers:
            pl.semaphore_signal(barrier, inc=1, device_id={"col": peer}, device_id_type=MESH)
        pl.semaphore_wait(barrier, 2 + len(peers))
        gb_all[me] = gb_ref[...]
        for k in range(nc - 1):
            gb_copy(k, me).start()

    each = -(-n // tiles)
    for at in range(tiles):
        @pl.when(step_now == at)
        def _():
            for step in range(at * each, min(n, (at + 1) * each)):
                w_step(step)

    hi, lo = split(j_ref[...])
    both = jnp.dot(jnp.concatenate([hi, lo], axis=0), vb_ref[...], preferred_element_type=F32)
    jv_tile = both[:tile, :K] + (both[:tile, K:] + both[tile:, :K]) + both[tile:, K:]
    total = jnp.zeros((tile, K), F32)
    for at in range(0, j_ref.shape[1], K):
        total = total + j_ref[:, at : at + K] * r_ref[:, at : at + K]
    jr_all[me, pl.ds(step_now, 1), :] = jnp.sum(jnp.transpose(total), axis=0, keepdims=True)
    jv[step_now] = jv_tile
    owner = step_now // per_share

    @pl.when(owner != me)
    def _():
        jv_copy(step_now, me, owner).start()

    @pl.when(owner == me)
    def _():
        rows = pl.ds(pl.multiple_of((step_now % per_share) * tile, tile), tile)
        jv_land[me, rows] = jv_tile

    @pl.when(step_now == tiles - 1)
    def _():
        for k in range(nc - 1):
            jr_copy(k, me).start()
        for k in range(nc - 1):
            gb_copy(k, peers[k]).wait_recv()
        sums = gb_all[0]
        for slot in range(1, nc):
            sums = sums + gb_all[slot]
        beta_ref[...] = sums[K:]
        gram = sums[:K]
        eye = (
            lax.broadcasted_iota(jnp.int32, (K, K), 0) == lax.broadcasted_iota(jnp.int32, (K, K), 1)
        ).astype(F32)
        trace = jnp.sum(jnp.sum(gram * eye, axis=0, keepdims=True), axis=1, keepdims=True)
        regular = gram + REG * (trace / K) * eye
        norm_one = jnp.max(
            jnp.sum(jnp.abs(regular), axis=0, keepdims=True), axis=1, keepdims=True
        )
        zmat = regular / (norm_one * norm_one)
        for sweep in range(NS):
            inner = jnp.dot(regular, zmat, precision=HIGH, preferred_element_type=F32)
            zmat = jnp.dot(zmat, 2.0 * eye - inner, precision=HIGH, preferred_element_type=F32)

        for k in range(nc - 1):
            for at in range(per_share):
                jv_copy(at, peers[k], me).wait_recv()
        for way in range(2):
            for part in range(parts):
                at = (way * parts + part) * grain
                jv_sum = jnp.zeros((grain, K), F32)
                for slot in range(nc):
                    jv_sum = jv_sum + jv_land[slot, at : at + grain]
                u_all[me, at : at + grain] = jnp.dot(
                    w_share[way, part] - jv_sum, zmat, precision=HIGH, preferred_element_type=F32
                )

        partner = me + 1 - 2 * (me % 2)

        def u_copy(slot, hop, peer):
            return to_col(
                u_all.at[slot], u_all.at[slot], u_send.at[hop], u_recv.at[slot], peer
            )

        half = nc // 2
        far = [(me + 2 * k) % nc for k in range(1, half)]
        for k, peer in enumerate(far):
            u_copy(me, k, peer).start()
        u_copy(me, half - 1, partner).start()
        for k in range(1, half):
            slot = (me + 2 * k) % nc
            u_copy(slot, half - 1 + k, partner).wait_recv()
            u_copy(slot, half - 1 + k, partner).start()

        for k in range(nc - 1):
            jr_copy(k, peers[k]).wait_recv()
        jr_sum = jr_all[0]
        for slot in range(1, nc):
            jr_sum = jr_sum + jr_all[slot]
        jr_ref[...] = jr_sum

        for k in range(half):
            slot = (partner + 2 * k) % nc
            u_copy(slot, 0, partner).wait_recv()
        u_ref[...] = u_all[...]
        for hop in range(nc - 1):
            u_copy(me, hop, partner).wait_send()
        for k in range(nc - 1):
            gb_copy(k, me).wait_send()
            jr_copy(k, me).wait_send()
            for at in range(per_share):
                jv_copy(peers[k] * per_share + at, me, peers[k]).wait_send()
        for step in range(n - 1):
            for part in range(parts):
                for way in range(2):
                    w_copy(step, way, part).wait_send()


def products(jacobian, vb, gb, residual, src, mask, x, grain, n, nc):
    rows, cols = jacobian.shape
    share = rows // nc
    tile = min(TILE, share)
    tiles = rows // tile
    parts = share // (2 * grain)
    dma = pltpu.SemaphoreType.DMA
    whole = lambda shape: pl.BlockSpec(shape, lambda i: (0,) * len(shape))
    out_shape = (
        jax.ShapeDtypeStruct((nc, share, K), F32),
        jax.ShapeDtypeStruct((8, K), F32),
        jax.ShapeDtypeStruct((tiles, tile), F32),
    )
    return pl.pallas_call(
        functools.partial(product_kernel, n, nc, parts),
        grid=(tiles,),
        out_shape=out_shape,
        in_specs=[
            SMEM_SPEC, SMEM_SPEC, VMEM_SPEC, VMEM_SPEC, VMEM_SPEC, VMEM_SPEC,
            pl.BlockSpec((tile, cols), lambda i: (i, 0)),
        ],
        out_specs=(VMEM_SPEC, VMEM_SPEC, VMEM_SPEC),
        scratch_shapes=[
            pltpu.VMEM((2, n - 1, parts, grain, K), F32),
            pltpu.VMEM((2, n - 1, parts, grain, K), F32),
            pltpu.VMEM((2, parts, grain, K), F32),
            pltpu.VMEM((tiles, tile, K), F32),
            pltpu.VMEM((nc, share, K), F32),
            pltpu.VMEM((nc, tiles, tile), F32),
            pltpu.VMEM((nc, K + 8, K), F32),
            pltpu.VMEM((nc, share, K), F32),
            dma((2, n - 1, parts)), dma((2, n - 1, parts)),
            dma((tiles,)), dma((nc, share // tile)),
            dma((nc - 1,)), dma((nc,)), dma((nc - 1,)), dma((nc,)),
            dma((nc - 1,)), dma((nc,)),
        ],
        compiler_params=pltpu.CompilerParams(collective_id=1, has_side_effects=True),
    )(src, mask, x.reshape(-1, grain, K), gb, residual, vb, jacobian)


def update_kernel(j_ref, u_ref, vt_ref, beta_ref, jr_ref, trial_ref, out_ref, corrected_ref):
    hi, lo = split(u_ref[...])
    twice = jnp.concatenate([hi, hi], axis=1)
    main = jnp.dot(twice, vt_ref[...], preferred_element_type=F32)
    rest = jnp.dot(lo, vt_ref[:K, :], preferred_element_type=F32)
    out_ref[...] = j_ref[...] + (main + rest)
    low_rank = jnp.sum(jnp.transpose(u_ref[...] * beta_ref[:1]), axis=0, keepdims=True)
    corrected_ref[...] = trial_ref[...] - (jr_ref[...] + low_rank)


def update(jacobian, u_rows, vt, beta, j_r, trial):
    rows, cols = jacobian.shape
    row = pl.BlockSpec((1, TILE), lambda i: (0, i))
    return pl.pallas_call(
        update_kernel,
        grid=(rows // TILE,),
        out_shape=(
            jax.ShapeDtypeStruct((rows, cols), F32),
            jax.ShapeDtypeStruct((1, rows), F32),
        ),
        in_specs=[
            pl.BlockSpec((TILE, cols), lambda i: (i, 0)),
            pl.BlockSpec((TILE, K), lambda i: (i, 0)),
            pl.BlockSpec((2 * K, cols), lambda i: (0, 0)),
            pl.BlockSpec((8, K), lambda i: (0, 0)),
            row,
            row,
        ],
        out_specs=(pl.BlockSpec((TILE, cols), lambda i: (i, 0)), row),
    )(jacobian, u_rows, vt, beta, j_r, trial)


def per_device(jacobian, diff_inputs, diff_outputs, face_dof, counts, residual, trial):
    row_block, col_block = jacobian.shape
    n_row, n_col = lax.axis_size("row"), lax.axis_size("col")
    col_at = lax.axis_index("col")
    runs = face_dof.shape[0] // UNIT
    first = jnp.arange(runs, dtype=jnp.int32) * UNIT
    run_unit = jnp.where(first < counts[0], face_dof.reshape(runs, UNIT)[:, 0] // UNIT, -1)

    part = min(UNIT, col_block // (2 * n_row))
    per_unit = UNIT // part
    granule = jnp.arange(col_block // part, dtype=jnp.int32)
    v_src, v_mask = lookup(run_unit, col_at * (col_block // UNIT) + granule // per_unit)
    v_src = v_src * per_unit + granule % per_unit

    share = row_block // n_col
    grain = min(UNIT, share // 2)
    per_share = share // grain
    piece = jnp.arange(n_row * per_share, dtype=jnp.int32)
    w_row = (piece // per_share) * row_block + col_at * share + (piece % per_share) * grain
    w_src, w_mask = lookup(run_unit, w_row // UNIT)
    w_src = w_src * (UNIT // grain) + (w_row % UNIT) // grain

    r_row = residual.reshape(1, col_block)
    vb, vt, gb = ring_sum(v_src, v_mask, diff_inputs, r_row, col_block, n_row)
    u, beta, j_r = products(
        jacobian, vb, gb, r_row, w_src, w_mask, diff_outputs, grain, n_row, n_col
    )
    updated, corrected = update(
        jacobian, u.reshape(row_block, K), vt, beta,
        j_r.reshape(1, row_block), trial.reshape(1, row_block),
    )
    return (updated, corrected[0])


def solution(mesh):
    placed = (
        P("row", "col"),
        P("row", None),
        P("row", None),
        P("row"),
        P("row"),
        P("col"),
        P("row"),
    )
    return jax.shard_map(
        per_device,
        mesh=mesh,
        in_specs=placed,
        out_specs=(P("row", "col"), P("row")),
        check_vma=False,
    )
```

time: 276 us -> 142 us (0.51)
  waiting for transfers between devices: 116 us -> 0 us
  Pallas kernels: 110 us -> 136 us
  between operations: 16.6 us -> 1.32 us
  blocking collectives: 10.9 us -> 0 us
  matrix products: 10.3 us -> 0 us
  other arithmetic: 9.29 us -> 2.55 us
    reduce_scatter x2 -> x0, waiting for transfers between devices: 88.7 us -> none  [the longest x1 72.5 us: per_device(): w_rows = lax.psum_scatter(w_piece, 'row', scatter_dimension=0, tiled=True)]
    psum x1 -> x0, waiting for transfers between devices: 26.2 us -> none  [per_device(): gram, beta, j_r = lax.psum((gram_part, beta_part, jr_part), 'col')]
    pallas_call x4 -> x3, Pallas kernels: 110 us -> 136 us  [the longest x1 61.9 us: ring_sum(): pl.pallas_call(functools.partial(ring_kernel, n, parts), out_shape=(jax.S...]
    psum x1 -> x0, blocking collectives: 10.9 us -> none  [per_device(): gram, beta, j_r = lax.psum((gram_part, beta_part, jr_part), 'col')]
    dot_general x10 -> x0, matrix products: 10.3 us -> none  [the longest x4 4.29 us: ns_inverse(): jnp.dot(regular, iterate, precision=HIGH)]
  transfers between devices with their start and end apart: 4 -> 0, of which waited for: 3 -> 0; matrix products, arithmetic and copies ran while one was open for 5% -> 0% of each run, Pallas kernels for 1% -> 0%
where the time goes in v2:
time: 142 us
  Pallas kernels  136 us (96%)
  other arithmetic  2.55 us (2%)
  local copies, waits for them, and re-layouts  2.12 us (1%)
    pallas_call x1, Pallas kernels, ring_sum(): pl.pallas_call(functools.partial(ring_kernel, n, parts), out_shape=(jax.S...  61.9 us
    pallas_call x1, Pallas kernels, products(): pl.pallas_call(functools.partial(product_kernel, n, nc, parts), grid=(til...  46.8 us
    pallas_call x1, Pallas kernels, update(): pl.pallas_call(update_kernel, grid=(rows // TILE,), out_shape=(jax.ShapeD...  26.9 us

profile of v2, /device:TPU:0, one launch (start us, length us, event | category | flops | bytes accessed | tf_op | source)
XLA Modules:
  0.0 141.6 jit_solution(5422645181254049116)
XLA Ops:
  1.3 0.8 slice_reduce_fusion
  2.1 0.2 compare_reduce_fusion
  2.3 0.7 fusion.1
  3.0 0.5 fusion.6.src_ref
  3.6 0.5 convert_element_type.7.mask_ref
  4.1 0.6 convert_element_type.6.mask_ref
  4.7 61.9 %shard_map.86 = (bf16[4096,256]{1,0:T(8,128)(2,1)}, bf16[256,4096]{1,0:T(8,128)(2,1)}, f32[136,128]{1,0:T(8,128)}) custom-call(s32[32]{0:T(128)} %get-tuple-element.20.src_ref, f32[32]{0:T(128)} %convert_element_type.7.mask_ref, f32[32,128,128]{2,1,0:T(8,128)} %bitcast.12, f32[1,4096]{1,0:T(1,128)} %bitcast.15), custom_call_target="tpu_custom_call" | custom-call | tf_op jit(solution)/shard_map/pallas_call | solution.py:126
  66.6 46.8 %shard_map.87 = (f32[4,512,128]{2,1,0:T(8,128)}, f32[8,128]{1,0:T(8,128)}, f32[8,256]{1,0:T(8,128)}) custom-call(s32[32]{0:T(128)} %fusion.6.src_ref, f32[32]{0:T(128)} %convert_element_type.6.mask_ref, f32[32,128,128]{2,1,0:T(8,128)} %bitcast.13, f32[136,128]{1,0:T(8,128)} %get-tuple-element.10.gb_ref, f32[1,4096]{1,0:T(1,128)} %bitcast.16, ...), custom_call_target="tpu_custom_call" | custom-call | tf_op jit(solution)/shard_map/pallas_call | solution.py:343
  113.4 1.3 copy.9
  114.7 26.9 %shard_map.88 = (f32[2048,4096]{1,0:T(8,128)}, f32[1,2048]{1,0:T(1,128)}) custom-call(f32[2048,4096]{1,0:T(8,128)} %j_ref.3, f32[2048,128]{1,0:T(8,128)} %bitcast.14, bf16[256,4096]{1,0:T(8,128)(2,1)} %get-tuple-element.13.vt_ref, f32[8,128]{1,0:T(8,128)} %get-tuple-element.14.beta_ref, f32[1,2048]{1,0:T(1,128)} %bitcast.17, f32[1,2048]{1,0:T(1,128)} %bitcast.19), custom_call_target="tpu_custom_call" | custom-call | tf_op jit(solution)/shard_map/pallas_call | solution.py:383
  (2 shorter events, 0.0 us)
